TPU v7x, 32 devices: a whole 2x2x4 slice. The times are simulated.
32 devices in a mesh: sample: 2 (over x), space: 16 (over z, y, core).
Axes of the slice: x: 2, y: 2, z: 4, core: 2. Of those that a mesh axis runs over, the one named last changes fastest.
Arguments:
- features: bfloat16 [2, 4, 128, 128, 128], P('sample', None, 'space'), parts along dimension 0, may hold values from -6 to 6
- log_perm: float32 [2, 128, 128, 128], P('sample', 'space'), parts along dimension 0, may hold values from -1.5 to 1.5
- well_cells: int32 [2, 32], P('sample'), parts along dimension 0, may hold values from 0 to 2097151
- well_rates: float32 [2, 32], P('sample'), parts along dimension 0, may hold values from 10 to 70
- lift_in: bfloat16 [5, 128], replicated, may hold values from -2.5 to 2.5
- lift_out: bfloat16 [128, 32], replicated, may hold values from -0.5 to 0.5
- spec_weight: bfloat16 [2, 1024, 32, 2048], P(None, 'space'), may hold values from -2 to 2
- point_weight: bfloat16 [2, 32, 32], replicated, may hold values from -1 to 1
- dec_in: bfloat16 [32, 64], replicated, may hold values from -1 to 1
- dec_out: bfloat16 [64, 2], replicated, may hold values from -0.75 to 0.75
Outputs:
- states: float32 [2, 2, 128, 128, 128], P('sample', None, 'space'), parts along dimension 0
- residual: float32 [2, 128, 128, 128], P('sample', 'space'), parts along dimension 0
There are 2 independent parts, one for each index of `sample`. A program takes and returns all parts, laid end to end along the dimension named above; an argument that names none is the same for every part. Nothing has to cross between parts.
Inputs may be any that keep to these rules, and one draw needn't show every extreme that they name: `well_cells`: cells of the sample's grid; several wells may share a cell.
All inputs are finite; a program needn't handle non-finite values.
Results may differ from a plain program's by a relative error of at most 0.03.
Values may be sent and summed in bfloat16 or wider, within the bound.
A program may use at most 192 MiB of HBM per device.

v0:
```python
import math

import jax
import jax.numpy as jnp
import numpy as np
from jax import lax
from jax.experimental import pallas as pl
from jax.experimental.pallas import tpu as pltpu
from jax.sharding import PartitionSpec as P

NX = 128
NY = 128
NZ = 128
MX = 32
MY = 32
MZ = 32
C = 32
FIN = 4
LAYERS = 2
WELLS = 32


def padded_2(block, sides, width):
    for axis, dim in sides:
        count = lax.axis_size(axis)
        forward = [(i, i + 1) for i in range(count - 1)]
        backward = [(target, source) for source, target in forward]
        low = lax.ppermute(
            lax.slice_in_dim(block, block.shape[dim] - width, None, axis=dim), axis, forward
        )
        high = lax.ppermute(lax.slice_in_dim(block, 0, width, axis=dim), axis, backward)
        block = jnp.concatenate([low, block, high], axis=dim)
    return block


def freq_table(length, kept, one_sided):
    indices = jnp.arange(kept, dtype=jnp.int32)
    if one_sided:
        return indices
    return jnp.where(indices < kept // 2, indices, length - kept + indices)


def wave_parts(length, kept, one_sided):
    freqs = freq_table(length, kept, one_sided)
    places = jnp.arange(length, dtype=jnp.int32)
    phase_turns = freqs[:, None] * places[None, :] % length
    angles = phase_turns.astype(jnp.float32) * (2.0 * math.pi / length)
    norm_scale = 1.0 / math.sqrt(length)
    return (jnp.cos(angles) * norm_scale, jnp.sin(angles) * norm_scale)


def forward_table(length, kept):
    cosine_vals, sine_vals = wave_parts(length, kept, False)
    return jnp.stack(
        [jnp.stack([cosine_vals.T, -sine_vals.T], 1), jnp.stack([sine_vals.T, cosine_vals.T], 1)], 1
    ).astype(jnp.bfloat16)


def inverse_table(length, kept):
    cosine_vals, sine_vals = wave_parts(length, kept, False)
    return jnp.stack(
        [jnp.stack([cosine_vals, sine_vals], 1), jnp.stack([-sine_vals, cosine_vals], 1)], 1
    ).astype(jnp.bfloat16)


def z_tables():
    cosine_vals, sine_vals = wave_parts(NZ, MZ, True)
    weights_k = jnp.where(jnp.arange(MZ) == 0, 1.0, 2.0).astype(jnp.float32)[:, None]
    z_forward = jnp.concatenate([cosine_vals.T, -sine_vals.T], 1).astype(jnp.bfloat16)
    z_inverse = jnp.concatenate([weights_k * cosine_vals, -weights_k * sine_vals], 0).astype(
        jnp.bfloat16
    )
    return (z_forward, z_inverse)


def gelu_tanh(values):
    return jax.nn.gelu(values, approximate=True)


def face_term(cond_a, cond_b, press_a, press_b):
    return 2.0 * cond_a * cond_b / (cond_a + cond_b) * (press_a - press_b)


def mobility_of(saturation, log_values):
    return jnp.exp(log_values) * (
        saturation * saturation + 0.5 * (1.0 - saturation) * (1.0 - saturation)
    )


def darcy(pressure, conduct, well_cells, well_rates):
    batches, planes = pressure.shape[0], pressure.shape[1]
    space_index = lax.axis_index("space")
    pad_cond = jnp.pad(conduct, ((0, 0), (0, 0), (1, 1), (1, 1)))
    pad_press = jnp.pad(pressure, ((0, 0), (0, 0), (1, 1), (1, 1)))
    flux_sum = face_term(conduct, pad_cond[:, :, 2:, 1:-1], pressure, pad_press[:, :, 2:, 1:-1])
    flux_sum = flux_sum + face_term(
        conduct, pad_cond[:, :, :-2, 1:-1], pressure, pad_press[:, :, :-2, 1:-1]
    )
    flux_sum = flux_sum + face_term(
        conduct, pad_cond[:, :, 1:-1, 2:], pressure, pad_press[:, :, 1:-1, 2:]
    )
    flux_sum = flux_sum + face_term(
        conduct, pad_cond[:, :, 1:-1, :-2], pressure, pad_press[:, :, 1:-1, :-2]
    )
    fields = jnp.stack([pressure, conduct], 1)
    padded = padded_2(fields.astype(jnp.bfloat16), (("space", 2),), 1).astype(fields.dtype)
    press_low = padded[:, 0, 0]
    press_high = padded[:, 0, -1]
    cond_low = padded[:, 1, 0]
    cond_high = padded[:, 1, -1]
    press_below = jnp.concatenate([press_low[:, None], pressure[:, :-1]], 1)
    cond_below = jnp.concatenate([cond_low[:, None], conduct[:, :-1]], 1)
    press_above = jnp.concatenate([pressure[:, 1:], press_high[:, None]], 1)
    cond_above = jnp.concatenate([conduct[:, 1:], cond_high[:, None]], 1)
    lower_terms = face_term(conduct, cond_below, pressure, press_below)
    upper_terms = face_term(conduct, cond_above, pressure, press_above)
    flux_sum = flux_sum + lower_terms + upper_terms
    well_x = well_cells // (NY * NZ) - space_index * planes
    well_y = well_cells // NZ % NY
    well_z = well_cells % NZ
    onehot_x = (well_x[:, :, None] == jnp.arange(planes, dtype=jnp.int32)[None, None, :]).astype(
        jnp.float32
    ) * well_rates[:, :, None]
    onehot_y = (well_y[:, :, None] == jnp.arange(NY, dtype=jnp.int32)[None, None, :]).astype(
        jnp.float32
    )
    onehot_z = (well_z[:, :, None] == jnp.arange(NZ, dtype=jnp.int32)[None, None, :]).astype(
        jnp.float32
    )
    plane_rows = (onehot_x[:, :, :, None] * onehot_y[:, :, None, :]).reshape(
        batches, WELLS, planes * NY
    )
    source = jnp.einsum(
        "bwa,bwz->baz", plane_rows, onehot_z, precision=lax.Precision.HIGHEST
    ).reshape(batches, planes, NY, NZ)
    return flux_sum - source


def local_general(
    features,
    log_perm,
    well_cells,
    well_rates,
    lift_in,
    lift_out,
    spec_weight,
    point_weight,
    dec_in,
    dec_out,
):
    batches = features.shape[0]
    planes = features.shape[2]
    space_index = lax.axis_index("space")
    block = spec_weight.shape[1]
    cell_count = planes * NY * NZ
    z_forward, z_inverse = z_tables()
    y_forward = forward_table(NY, MY)
    y_inverse = inverse_table(NY, MY)
    x_forward = forward_table(NX, MX)
    x_inverse = inverse_table(NX, MX)
    perm_b = log_perm.astype(jnp.bfloat16).reshape(batches, 1, cell_count)
    lift_input = jnp.concatenate([features.reshape(batches, FIN, cell_count), perm_b], 1)
    lift_hidden = jnp.einsum("bfn,fh->bhn", lift_input, lift_in, preferred_element_type=jnp.float32)
    lifted = gelu_tanh(lift_hidden).astype(jnp.bfloat16)
    hidden_state = jnp.einsum(
        "bhn,hc->bcn", lifted, lift_out, preferred_element_type=jnp.float32
    ).astype(jnp.bfloat16)
    for layer_idx in range(LAYERS):
        zspec = jnp.dot(hidden_state.reshape(-1, NZ), z_forward, preferred_element_type=jnp.float32)
        zspec = zspec.astype(jnp.bfloat16).reshape(batches * C * planes, NY, 2, MZ)
        yz_spec = jnp.einsum(
            "aypk,ypqj->aqjk", zspec, y_forward, preferred_element_type=jnp.float32
        )
        yz_spec = yz_spec.astype(jnp.bfloat16).reshape(batches, C, planes, 2, MY * MZ)
        mode_weights = spec_weight[layer_idx].reshape(block, C, MX, 2, C)
        spectrum = jnp.einsum(
            "bcxpm,xpqi->bcqim",
            lax.all_to_all(yz_spec, "space", split_axis=4, concat_axis=2, tiled=True),
            x_forward,
            preferred_element_type=jnp.float32,
        ).astype(jnp.bfloat16)
        products = jnp.einsum(
            "bcqim,mcipo->bimqpo", spectrum, mode_weights, preferred_element_type=jnp.float32
        )
        real_part = products[:, :, :, 0, 0] - products[:, :, :, 1, 1]
        imag_part = products[:, :, :, 0, 1] + products[:, :, :, 1, 0]
        mixed_modes = jnp.stack([real_part, imag_part], 3).astype(jnp.bfloat16)
        back_field = jnp.einsum(
            "bimqo,iqpx->boxpm", mixed_modes, x_inverse, preferred_element_type=jnp.float32
        ).astype(jnp.bfloat16)
        returned = lax.all_to_all(back_field, "space", split_axis=2, concat_axis=4, tiled=True)
        returned = returned.reshape(batches * C * planes, 2, MY, MZ)
        y_back = jnp.einsum(
            "aqjk,jqpy->aypk", returned, y_inverse, preferred_element_type=jnp.float32
        ).astype(jnp.bfloat16)
        spectral = jnp.dot(
            y_back.reshape(-1, 2 * MZ), z_inverse, preferred_element_type=jnp.float32
        ).reshape(batches, C, cell_count)
        local_term = jnp.einsum(
            "bcn,co->bon", hidden_state, point_weight[layer_idx], preferred_element_type=jnp.float32
        )
        hidden_state = gelu_tanh(spectral + local_term).astype(jnp.bfloat16)
    decoded = gelu_tanh(
        jnp.einsum("bcn,cd->bdn", hidden_state, dec_in, preferred_element_type=jnp.float32)
    ).astype(jnp.bfloat16)
    decoded_out = jnp.einsum("bdn,de->ben", decoded, dec_out, preferred_element_type=jnp.float32)
    pressure = decoded_out[:, 0].reshape(batches, planes, NY, NZ)
    saturation = jax.nn.sigmoid(decoded_out[:, 1]).reshape(batches, planes, NY, NZ)
    states = jnp.stack([pressure, saturation], 1)
    conduct = mobility_of(saturation, log_perm)
    return (states, darcy(pressure, conduct, well_cells, well_rates))


BF = jnp.bfloat16
F32 = jnp.float32
PAIRS = NY // 2
PITCH = PAIRS + 8
MODE_STEP = 8
ROWS = 8
LANES = 128


def np_waves(length, kept, one_sided):
    index = np.arange(kept)
    freqs = index if one_sided else np.where(index < kept // 2, index, length - kept + index)
    angles = (freqs[:, None] * np.arange(length)[None, :] % length) * (2.0 * math.pi / length)
    norm = 1.0 / math.sqrt(length)
    return np.cos(angles) * norm, np.sin(angles) * norm


def np_forward(length, kept):
    cosine, sine = np_waves(length, kept, False)
    return np.stack([np.stack([cosine.T, -sine.T], 1), np.stack([sine.T, cosine.T], 1)], 1)


def np_inverse(length, kept):
    cosine, sine = np_waves(length, kept, False)
    return np.stack([np.stack([cosine, sine], 1), np.stack([-sine, cosine], 1)], 1)


def tables_for(count):
    own = MY // count
    cosine, sine = np_waves(NZ, MZ, True)
    twice = np.where(np.arange(MZ) == 0, 1.0, 2.0)[:, None]
    z_forward = np.concatenate([cosine.T, -sine.T], 1)
    z_inverse = np.concatenate([twice * cosine, -twice * sine], 0)
    y_forward = np_forward(NY, MY).reshape(PAIRS, 2, 2, 2, count, own)
    y_inverse = np_inverse(NY, MY).reshape(count, own, 2, 2, PAIRS, 2)
    pair = np.eye(2)
    tables = {
        "zf": np.kron(pair, z_forward),
        "zi": np.kron(pair, z_inverse),
        "yf": y_forward.transpose(3, 5, 4, 1, 2, 0).reshape(2 * MY, 2 * NY),
        "yi": y_inverse.transpose(5, 3, 4, 2, 1, 0).reshape(2 * NY, 2 * MY),
        "xf": np_forward(NX, MX).transpose(1, 2, 3, 0).reshape(2, 2 * MX, NX),
        "xi": np_inverse(NX, MX).transpose(2, 3, 0, 1).reshape(2, NX, 2 * MX),
    }
    return {name: jnp.asarray(table.astype(np.float32)).astype(BF) for name, table in tables.items()}


def dot32(a, b):
    return jnp.dot(a, b, preferred_element_type=F32)


def gelu_fast(values):
    v = values.astype(BF)
    scale = math.sqrt(2.0 / math.pi)
    inner = v * (BF(scale) + BF(scale * 0.044715) * (v * v))
    half = BF(0.5) * v
    return half + half * jnp.tanh(inner)


def swap_blocks(four):
    shape = four[0].shape
    lane = lax.broadcasted_iota(jnp.int32, shape, 1)
    low = lane < 64
    even = lane % 64 < 32
    a0, a1, a2, a3 = four

    def cross(a, b, keep, shift):
        return (
            jnp.where(keep, a, pltpu.roll(b, shift, 1)),
            jnp.where(keep, pltpu.roll(a, LANES - shift, 1), b),
        )

    b0, b2 = cross(a0, a2, low, 64)
    b1, b3 = cross(a1, a3, low, 64)
    c0, c1 = cross(b0, b1, even, 32)
    c2, c3 = cross(b2, b3, even, 32)
    return c0, c1, c2, c3


def to_modes(plane, planes, count, yf_ref, zs, send, out_ref):
    pieces = []
    for group in range(C // 4):
        four = [zs[(group * 4 + r) * PITCH : (group * 4 + r) * PITCH + PAIRS, :] for r in range(4)]
        pieces.append(jnp.concatenate([p.astype(BF) for p in swap_blocks(four)], 0))
    stacked = jnp.concatenate(pieces, 1)
    modes = dot32(yf_ref[...], stacked)
    tiles = C * MZ // LANES
    for s in range(2 * MY // count):
        for t in range(tiles):
            send[s * tiles + t, pl.ds(plane, count, stride=planes), :] = modes[
                s * count : (s + 1) * count, t * LANES : (t + 1) * LANES
            ]

    @pl.when(plane == planes - 1)
    def _():
        for t in range(send.shape[0]):
            out_ref[:, t * LANES : (t + 1) * LANES] = send[t].astype(BF)


def lay_out(zs, start, values):
    for r in range(ROWS):
        zs[pl.ds(start + r, C, stride=PITCH), :] = values[r * C : (r + 1) * C, :]


def lift_kernel(
    planes, count, feat_ref, perm_ref, in_ref, lo_ref, zf_ref, yf_ref, hid_ref, out_ref, plain, xs, zs, send
):
    plane = pl.program_id(0)

    @pl.when(plane == 0)
    def _():
        xs[...] = jnp.zeros_like(xs)

    for f in range(FIN + 1):
        plain[...] = perm_ref[0, 0] if f == FIN else feat_ref[0, f, 0].astype(F32)
        for y2 in range(2):
            xs[y2, pl.ds(f, PAIRS, stride=8), :] = plain[pl.ds(y2, PAIRS, stride=2), :]
    width = lo_ref.shape[1]

    def block(index, carry):
        start = pl.multiple_of(index * ROWS * 8, ROWS * 8)
        x = jnp.concatenate([xs[0, pl.ds(start, ROWS * 8), :], xs[1, pl.ds(start, ROWS * 8), :]], 1)
        lifted = gelu_fast(dot32(in_ref[...], x.astype(BF)))
        parts = [
            dot32(lo_ref[...], lifted[r * width : (r + 1) * width, :]).astype(BF)
            for r in range(lifted.shape[0] // width)
        ]
        hidden = jnp.concatenate(parts, 0)
        hid_ref[0, pl.ds(pl.multiple_of(index * ROWS * C, ROWS * C), ROWS * C), :] = hidden
        lay_out(zs, index * ROWS, dot32(hidden, zf_ref[...]))
        return carry

    lax.fori_loop(0, PAIRS // ROWS, block, 0)
    to_modes(plane, planes, count, yf_ref, zs, send, out_ref)


def from_modes(plane, planes, count, got_ref, yi_ref, recv, zs):
    @pl.when(plane == 0)
    def _():
        for t in range(recv.shape[0]):
            recv[t] = got_ref[:, t * LANES : (t + 1) * LANES].astype(F32)

    tiles = C * MZ // LANES
    rows = []
    for s in range(2 * MY // count):
        rows.append(
            jnp.concatenate(
                [recv[s * tiles + t, pl.ds(plane, count, stride=planes), :] for t in range(tiles)], 1
            ).astype(BF)
        )
    back = dot32(yi_ref[...], jnp.concatenate(rows, 0))
    for group in range(C // 4):
        lanes = slice(group * LANES, (group + 1) * LANES)
        four = [back[g * PAIRS : (g + 1) * PAIRS, lanes] for g in range(4)]
        for r, piece in enumerate(swap_blocks(four)):
            zs[(group * 4 + r) * PITCH : (group * 4 + r) * PITCH + PAIRS, :] = piece


def layer_rows(index, zs, hid_ref, zi_ref, kp_ref):
    start = index * ROWS
    parts = [zs[pl.ds(start + r, C, stride=PITCH), :].astype(BF) for r in range(ROWS)]
    spectral = dot32(jnp.concatenate(parts, 0), zi_ref[...])
    old = hid_ref[0, pl.ds(pl.multiple_of(index * ROWS * C, ROWS * C), ROWS * C), :]
    return gelu_fast(spectral + dot32(kp_ref[...], old))


def middle_kernel(
    planes, count, got_ref, hid_ref, kp_ref, yi_ref, zi_ref, zf_ref, yf_ref, new_ref, out_ref, recv, zs, zs2, send
):
    plane = pl.program_id(0)
    from_modes(plane, planes, count, got_ref, yi_ref, recv, zs)

    def block(index, carry):
        hidden = layer_rows(index, zs, hid_ref, zi_ref, kp_ref)
        new_ref[0, pl.ds(pl.multiple_of(index * ROWS * C, ROWS * C), ROWS * C), :] = hidden
        lay_out(zs2, index * ROWS, dot32(hidden, zf_ref[...]))
        return carry

    lax.fori_loop(0, PAIRS // ROWS, block, 0)
    to_modes(plane, planes, count, yf_ref, zs2, send, out_ref)


def final_kernel(
    planes, count, got_ref, hid_ref, kp_ref, yi_ref, zi_ref, di_ref, do_ref, perm_ref, st_ref, cond_ref, recv, zs
):
    plane = pl.program_id(0)
    from_modes(plane, planes, count, got_ref, yi_ref, recv, zs)

    def block(index, carry):
        hidden = layer_rows(index, zs, hid_ref, zi_ref, kp_ref)
        decoded = gelu_fast(dot32(di_ref[...], hidden))
        both = dot32(do_ref[...], decoded)
        for y2 in range(2):
            lanes = slice(y2 * NZ, (y2 + 1) * NZ)
            where = pl.ds(index * ROWS * 2 + y2, ROWS, stride=2)
            st_ref[0, 0, 0, where, :] = both[:ROWS, lanes]
            st_ref[0, 1, 0, where, :] = both[ROWS:, lanes]
        return carry

    lax.fori_loop(0, PAIRS // ROWS, block, 0)
    sat = jax.nn.sigmoid(st_ref[0, 1, 0])
    st_ref[0, 1, 0] = sat
    cond_ref[0, 0] = mobility_of(sat, perm_ref[0, 0])


def mix_kernel(own, a_ref, w_ref, xf_ref, xi_ref, out_ref, spec, mixed, turned, rhs):
    step = pl.program_id(0)
    half = C * own * MZ
    wide = MX * 2 * C

    @pl.when(step == 0)
    def _():
        total = dot32(xf_ref[0], a_ref[:, :half]) + dot32(xf_ref[1], a_ref[:, half:])
        spec[:, : 2 * MX] = total.T

    first = step * MODE_STEP
    base = first // MZ * (C * MZ) + first % MZ
    rows = [spec[pl.ds(base + r, C, stride=MZ), :] for r in range(MODE_STEP)]
    values = jnp.concatenate(rows, 0)[:, : 2 * MX].astype(BF)
    chunk = 512
    for piece in range(wide // chunk):
        lo = piece * chunk
        row = lax.broadcasted_iota(jnp.int32, (2 * MX, chunk), 0)
        col = lax.broadcasted_iota(jnp.int32, (2 * MX, chunk), 1) + lo
        weights = w_ref[0, :, :, lo : lo + chunk].reshape(MODE_STEP * C, chunk).astype(F32)
        sums = []
        for q in range(2):
            pick = jnp.where(row == col // (2 * C) + q * MX, 1.0, 0.0).astype(BF)
            terms = dot32(values, pick) * weights
            sums.append(jnp.sum(terms.reshape(MODE_STEP, C, chunk), 1))
        lane = lax.broadcasted_iota(jnp.int32, (MODE_STEP, chunk), 1)
        turn = jnp.where(
            lane % (2 * C) < C, -pltpu.roll(sums[1], chunk - C, 1), pltpu.roll(sums[1], C, 1)
        )
        mixed[pl.ds(pl.multiple_of(first, MODE_STEP), MODE_STEP), lo : lo + chunk] = sums[0] + turn

    @pl.when(step == pl.num_programs(0) - 1)
    def _():
        modes = own * MZ
        turned[:, :modes] = mixed[...].T
        for o in range(C):
            piece = turned[pl.ds(o, 2 * MX, stride=C), :]
            for jj in range(own):
                lo = (jj * C + o) * MZ
                rhs[:, lo : lo + MZ] = piece[:, jj * MZ : (jj + 1) * MZ]
        right = rhs[...].astype(BF)
        for p in range(2):
            out_ref[:, p * half : (p + 1) * half] = dot32(xi_ref[p], right).astype(BF)


def whole_spec(array):
    dims = array.ndim
    return pl.BlockSpec(array.shape, lambda i: (0,) * dims)


def block_diag(matrix, copies):
    rows, cols = matrix.shape
    eye = jnp.eye(copies, dtype=matrix.dtype)
    return (eye[:, None, :, None] * matrix[None, :, None, :]).reshape(copies * rows, copies * cols)


def local_fast(
    features,
    log_perm,
    well_cells,
    well_rates,
    lift_in,
    lift_out,
    spec_weight,
    point_weight,
    dec_in,
    dec_out,
):
    planes = features.shape[2]
    count = lax.axis_size("space")
    own = MY // count
    tables = tables_for(count)
    params = pltpu.CompilerParams(
        dimension_semantics=("arbitrary",), vmem_limit_bytes=56 * 1024 * 1024
    )
    sends = 2 * own * C * MZ
    tiles = sends // LANES
    hid_shape = jax.ShapeDtypeStruct((planes, PAIRS * C, 2 * NZ), BF)
    send_shape = jax.ShapeDtypeStruct((count * planes, sends), BF)
    hid_spec = pl.BlockSpec((1, PAIRS * C, 2 * NZ), lambda i: (i, 0, 0))
    send_spec = pl.BlockSpec((count * planes, sends), lambda i: (0, 0))
    zs_scratch = pltpu.VMEM((C * PITCH, LANES), F32)
    send_scratch = pltpu.VMEM((tiles, count * planes, LANES), F32)
    perm_spec = pl.BlockSpec((1, 1, NY, NZ), lambda i: (0, i, 0, 0))
    in_rows = jnp.pad(lift_in, ((0, 8 - FIN - 1), (0, 0))).T
    k_in = block_diag(in_rows, ROWS)
    k_lo = block_diag(lift_out.T, 2)
    k_di = block_diag(dec_in.T, ROWS)
    eye = jnp.eye(ROWS, dtype=BF)
    k_do = (dec_out.T[:, None, None, :] * eye[None, :, :, None]).reshape(2 * ROWS, -1)

    def swap(sent):
        return lax.all_to_all(
            sent.reshape(count, planes, sends), "space", split_axis=0, concat_axis=0, tiled=True
        ).reshape(count * planes, sends)

    operands = (features, log_perm, k_in, k_lo, tables["zf"], tables["yf"])
    hidden, sent = pl.pallas_call(
        lambda *refs: lift_kernel(planes, count, *refs),
        grid=(planes,),
        in_specs=[pl.BlockSpec((1, FIN, 1, NY, NZ), lambda i: (0, 0, i, 0, 0)), perm_spec]
        + [whole_spec(a) for a in operands[2:]],
        out_specs=[hid_spec, send_spec],
        out_shape=[hid_shape, send_shape],
        scratch_shapes=[
            pltpu.VMEM((NY, NZ), F32),
            pltpu.VMEM((2, PAIRS * 8, NZ), F32),
            zs_scratch,
            send_scratch,
        ],
        compiler_params=params,
        name="lift",
    )(*operands)
    for layer_idx in range(LAYERS):
        arrived = swap(sent)
        modes = own * MZ
        mixed = pl.pallas_call(
            lambda *refs: mix_kernel(own, *refs),
            grid=(modes // MODE_STEP,),
            in_specs=[
                send_spec,
                pl.BlockSpec(
                    (1, MODE_STEP, C, MX * 2 * C), lambda i, layer=layer_idx: (layer, i, 0, 0)
                ),
                whole_spec(tables["xf"]),
                whole_spec(tables["xi"]),
            ],
            out_specs=send_spec,
            out_shape=send_shape,
            scratch_shapes=[
                pltpu.VMEM((modes * C, LANES), F32),
                pltpu.VMEM((modes, MX * 2 * C), F32),
                pltpu.VMEM((MX * 2 * C, LANES), F32),
                pltpu.VMEM((2 * MX, modes * C), F32),
            ],
            compiler_params=params,
            name="mix",
        )(arrived, spec_weight, tables["xf"], tables["xi"])
        returned = swap(mixed)
        k_p = block_diag(point_weight[layer_idx].T, ROWS)
        shared = (returned, hidden, k_p, tables["yi"], tables["zi"])
        shared_specs = [send_spec, hid_spec] + [whole_spec(a) for a in shared[2:]]
        if layer_idx < LAYERS - 1:
            operands = shared + (tables["zf"], tables["yf"])
            hidden, sent = pl.pallas_call(
                lambda *refs: middle_kernel(planes, count, *refs),
                grid=(planes,),
                in_specs=shared_specs + [whole_spec(a) for a in operands[5:]],
                out_specs=[hid_spec, send_spec],
                out_shape=[hid_shape, send_shape],
                scratch_shapes=[send_scratch, zs_scratch, zs_scratch, send_scratch],
                compiler_params=params,
                name="middle",
            )(*operands)
        else:
            states, conduct = pl.pallas_call(
                lambda *refs: final_kernel(planes, count, *refs),
                grid=(planes,),
                in_specs=shared_specs + [whole_spec(k_di), whole_spec(k_do), perm_spec],
                out_specs=[pl.BlockSpec((1, 2, 1, NY, NZ), lambda i: (0, 0, i, 0, 0)), perm_spec],
                out_shape=[
                    jax.ShapeDtypeStruct((1, 2, planes, NY, NZ), F32),
                    jax.ShapeDtypeStruct((1, planes, NY, NZ), F32),
                ],
                scratch_shapes=[send_scratch, zs_scratch],
                compiler_params=params,
                name="final",
            )(*shared, k_di, k_do, log_perm)
    return (states, darcy(states[:, 0], conduct, well_cells, well_rates))


def local(features, log_perm, well_cells, well_rates, lift_in, lift_out, spec_weight, *rest):
    batches, planes = features.shape[0], features.shape[2]
    count = lax.axis_size("space")
    fits = batches == 1 and planes == 8 and count % 8 == 0 and MY % count == 0
    run = local_fast if fits else local_general
    return run(
        features, log_perm, well_cells, well_rates, lift_in, lift_out, spec_weight, *rest
    )


def solution(mesh):
    return jax.shard_map(
        local,
        mesh=mesh,
        in_specs=(
            P("sample", None, "space", None, None),
            P("sample", "space", None, None),
            P("sample", None),
            P("sample", None),
            P(),
            P(),
            P(None, "space", None, None),
            P(),
            P(),
            P(),
        ),
        out_specs=(P("sample", None, "space", None, None), P("sample", "space", None, None)),
        check_vma=False,
    )
```

profile of v0, /device:TPU:13, one launch (start us, length us, event | category | flops | bytes accessed | tf_op | source)
XLA Modules:
  0.0 320.7 jit_solution(3276292515453988419)
XLA Ops:
  3.7 52.1 %lift.1 = (bf16[8,2048,256]{2,1,0:T(8,128)(2,1)}, bf16[128,4096]{1,0:T(8,128)(2,1)}) custom-call(bf16[1,4,8,128,128]{4,3,2,1,0:T(8,128)(2,1)} %refs_0_.1, f32[1,8,128,128]{3,2,1,0:T(8,128)} %refs_7_.1, bf16[1024,64]{1,0:T(8,128)(2,1)} %copy.22.refs_2_, bf16[64,256]{1,0:T(8,128)(2,1)} %bitcast.98, bf16[256,128]{1,0:T(8,128)(2,1)} %constant.86.refs_4_.refs_5_, ...), custom_call_target="tpu_custom_call" | custom-call | tf_op jit(solution)/shard_map/lift/pallas_call | solution.py:516
  55.8 31.4 %all_to_all.20 = bf16[16,8,4096]{2,1,0:T(8,128)(2,1)} all-to-all(bf16[16,8,4096]{2,1,0:T(8,128)(2,1)} %bitcast.96), channel_id=1, replica_groups=mesh['sample'=2,'space'=16] {'space'}, dimensions={0} | all-to-all | bytes 2097152 | tf_op jit(solution)/shard_map/all_to_all | solution.py:511
  87.2 13.1 %mix.2 = bf16[128,4096]{1,0:T(8,128)(2,1)} custom-call(bf16[128,4096]{1,0:T(8,128)(2,1)} %bitcast.94, bf16[2,64,32,2048]{3,2,1,0:T(8,128)(2,1)} %refs_1_.5, bf16[2,64,128]{2,1,0:T(8,128)(2,1)} %constant.88.refs_2_, bf16[2,128,64]{2,1,0:T(8,128)(2,1)} %constant.89.refs_3_), custom_call_target="tpu_custom_call" | custom-call | tf_op jit(solution)/shard_map/mix/pallas_call | solution.py:535
  100.3 4.9 %all-to-all-start.1 = ((bf16[16,8,4096]{2,1,0:T(8,128)(2,1)}), bf16[16,8,4096]{2,1,0:T(8,128)(2,1)S(1)}, u32[]{:S(2)}, u32[]{:S(2)}) async-start(bf16[16,8,4096]{2,1,0:T(8,128)(2,1)} %bitcast.92), calls=%async_computation.1 | async-start | bytes 2097152 | tf_op jit(solution)/shard_map/all_to_all | solution.py:511
  105.7 1.0 mul.190.refs_2_
  106.7 23.4 %all-to-all-done.1 = bf16[16,8,4096]{2,1,0:T(8,128)(2,1)S(1)} async-done(((bf16[16,8,4096]{2,1,0:T(8,128)(2,1)}), bf16[16,8,4096]{2,1,0:T(8,128)(2,1)S(1)}, u32[]{:S(2)}, u32[]{:S(2)}) %all-to-all-start.1) | async-done | bytes 1048608 | tf_op jit(solution)/shard_map/all_to_all | solution.py:511
  130.1 1.0 copy-done.2
  131.1 44.5 %middle.1 = (bf16[8,2048,256]{2,1,0:T(8,128)(2,1)}, bf16[128,4096]{1,0:T(8,128)(2,1)}) custom-call(bf16[128,4096]{1,0:T(8,128)(2,1)} %bitcast.91, bf16[8,2048,256]{2,1,0:T(8,128)(2,1)} %get-tuple-element.9.refs_1_, bf16[256,256]{1,0:T(8,128)(2,1)} %mul.190.refs_2_, bf16[256,64]{1,0:T(8,128)(2,1)} %constant.90.refs_3_, bf16[128,256]{1,0:T(8,128)(2,1)} %constant.91.refs_4_, ...), custom_call_target="tpu_custom_call" | custom-call | tf_op jit(solution)/shard_map/middle/pallas_call | solution.py:563
  175.6 29.7 %all_to_all.21 = bf16[16,8,4096]{2,1,0:T(8,128)(2,1)} all-to-all(bf16[16,8,4096]{2,1,0:T(8,128)(2,1)} %bitcast.95), channel_id=1, replica_groups=mesh['sample'=2,'space'=16] {'space'}, dimensions={0} | all-to-all | bytes 2097152 | tf_op jit(solution)/shard_map/all_to_all | solution.py:511
  205.4 13.1 %mix.3 = bf16[128,4096]{1,0:T(8,128)(2,1)} custom-call(bf16[128,4096]{1,0:T(8,128)(2,1)} %bitcast.93, bf16[2,64,32,2048]{3,2,1,0:T(8,128)(2,1)} %refs_1_.5, bf16[2,64,128]{2,1,0:T(8,128)(2,1)} %constant.88.refs_2_, bf16[2,128,64]{2,1,0:T(8,128)(2,1)} %constant.89.refs_3_), custom_call_target="tpu_custom_call" | custom-call | tf_op jit(solution)/shard_map/mix/pallas_call | solution.py:535
  218.5 4.9 %all-to-all-start.3 = ((bf16[16,8,4096]{2,1,0:T(8,128)(2,1)}), bf16[16,8,4096]{2,1,0:T(8,128)(2,1)S(1)}, u32[]{:S(2)}, u32[]{:S(2)}) async-start(bf16[16,8,4096]{2,1,0:T(8,128)(2,1)} %bitcast.90), calls=%async_computation.3 | async-start | bytes 2097152 | tf_op jit(solution)/shard_map/all_to_all | solution.py:511
  223.4 1.0 mul.193.refs_2_
  226.7 21.5 %all-to-all-done.3 = bf16[16,8,4096]{2,1,0:T(8,128)(2,1)S(1)} async-done(((bf16[16,8,4096]{2,1,0:T(8,128)(2,1)}), bf16[16,8,4096]{2,1,0:T(8,128)(2,1)S(1)}, u32[]{:S(2)}, u32[]{:S(2)}) %all-to-all-start.3) | async-done | bytes 1048608 | tf_op jit(solution)/shard_map/all_to_all | solution.py:511
  248.2 1.1 copy-done.1
  249.3 54.4 %final.1 = (f32[1,2,8,128,128]{4,3,2,1,0:T(8,128)}, f32[1,8,128,128]{3,2,1,0:T(8,128)}) custom-call(bf16[128,4096]{1,0:T(8,128)(2,1)} %bitcast.89, bf16[8,2048,256]{2,1,0:T(8,128)(2,1)} %get-tuple-element.11.refs_1_, bf16[256,256]{1,0:T(8,128)(2,1)} %mul.193.refs_2_, bf16[256,64]{1,0:T(8,128)(2,1)} %constant.90.refs_3_, bf16[128,256]{1,0:T(8,128)(2,1)} %constant.91.refs_4_, ...), custom_call_target="tpu_custom_call" | custom-call | tf_op jit(solution)/shard_map/final/pallas_call | solution.py:574
  303.7 1.1 convert_bitcast_fusion.4
  304.8 1.1 convert.12
  305.9 1.1 fusion.31
  307.0 1.1 slice_bitcast_fusion
  308.1 3.7 %collective-permute-start = (bf16[1,2,1,128,128]{4,3,2,1,0:T(8,128)(2,1)S(1)}, bf16[1,2,1,128,128]{4,3,2,1,0:T(8,128)(2,1)S(1)}, u32[]{:S(2)}, u32[]{:S(2)}) collective-permute-start(bf16[1,2,1,128,128]{4,3,2,1,0:T(8,128)(2,1)S(1)} %get-tuple-element.24), channel_id=1, source_target_pairs={{0,1},{1,2},{2,3},{3,4},{4,5},{5,6},{6,7},{7,8},{8,9},{9,10},{10,1... | collective-permute-start | bytes 196616 | tf_op jit(solution)/shard_map/ppermute | solution.py:28
  311.8 1.9 collective-permute-start.1
  313.7 1.4 fusion.32
  315.2 3.1 collective-permute-done.1
  318.3 2.4 fusion
  (40 shorter events, 5.9 us)
Async XLA Ops:
  87.2 18.1 %copy-start.3 = (bf16[2,32,32]{2,1,0:T(8,128)(2,1)S(1)}, bf16[2,32,32]{2,1,0:T(8,128)(2,1)}, u32[]{:S(2)}) copy-start(bf16[2,32,32]{2,1,0:T(8,128)(2,1)} %param.23) | copy-start | bytes 12292
  100.3 29.8 %all-to-all-start.1 = ((bf16[16,8,4096]{2,1,0:T(8,128)(2,1)}), bf16[16,8,4096]{2,1,0:T(8,128)(2,1)S(1)}, u32[]{:S(2)}, u32[]{:S(2)}) async-start(bf16[16,8,4096]{2,1,0:T(8,128)(2,1)} %bitcast.92), calls=%async_computation.1 | async-start | bytes 2097152 | tf_op jit(solution)/shard_map/all_to_all | solution.py:511
  130.1 1.0 copy-start.2
  205.3 19.1 %copy-start.5 = (bf16[64,2]{0,1:T(2,128)(2,1)S(1)}, bf16[64,2]{0,1:T(2,128)(2,1)}, u32[]{:S(2)}) copy-start(bf16[64,2]{0,1:T(2,128)(2,1)} %param.25) | copy-start | bytes 772
  205.4 19.8 %copy-start.4 = (bf16[32,64]{1,0:T(8,128)(2,1)S(1)}, bf16[32,64]{1,0:T(8,128)(2,1)}, u32[]{:S(2)}) copy-start(bf16[32,64]{1,0:T(8,128)(2,1)} %param.24) | copy-start | bytes 12292
  205.4 21.1 %copy-start.6 = (s32[1,32]{1,0:T(1,128)S(1)}, s32[1,32]{1,0:T(1,128)}, u32[]{:S(2)}) copy-start(s32[1,32]{1,0:T(1,128)} %param.18) | copy-start | bytes 388
  205.4 21.2 %copy-start.7 = (f32[1,32]{1,0:T(1,128)S(1)}, f32[1,32]{1,0:T(1,128)}, u32[]{:S(2)}) copy-start(f32[1,32]{1,0:T(1,128)} %param.19) | copy-start | bytes 388
  218.5 29.8 %all-to-all-start.3 = ((bf16[16,8,4096]{2,1,0:T(8,128)(2,1)}), bf16[16,8,4096]{2,1,0:T(8,128)(2,1)S(1)}, u32[]{:S(2)}, u32[]{:S(2)}) async-start(bf16[16,8,4096]{2,1,0:T(8,128)(2,1)} %bitcast.90), calls=%async_computation.3 | async-start | bytes 2097152 | tf_op jit(solution)/shard_map/all_to_all | solution.py:511
  248.2 1.1 copy-start.1
  303.7 14.6 %copy-start = (f32[1,8,128,128]{3,2,1,0:T(8,128)S(1)}, f32[1,8,128,128]{3,2,1,0:T(8,128)}, u32[]{:S(2)}) copy-start(f32[1,8,128,128]{3,2,1,0:T(8,128)} %get-tuple-element.13) | copy-start | bytes 1572868
  308.1 7.0 %collective-permute-start = (bf16[1,2,1,128,128]{4,3,2,1,0:T(8,128)(2,1)S(1)}, bf16[1,2,1,128,128]{4,3,2,1,0:T(8,128)(2,1)S(1)}, u32[]{:S(2)}, u32[]{:S(2)}) collective-permute-start(bf16[1,2,1,128,128]{4,3,2,1,0:T(8,128)(2,1)S(1)} %get-tuple-element.24), channel_id=1, source_target_pairs={{0,1},{1,2},{2,3},{3,4},{4,5},{5,6},{6,7},{7,8},{8,9},{9,10},{10,1... | collective-permute-start | bytes 196616 | tf_op jit(solution)/shard_map/ppermute | solution.py:28
  311.8 6.5 %collective-permute-start.1 = (bf16[1,2,1,128,128]{4,3,2,1,0:T(8,128)(2,1)S(1)}, bf16[1,2,1,128,128]{4,3,2,1,0:T(8,128)(2,1)S(1)}, u32[]{:S(2)}, u32[]{:S(2)}) collective-permute-start(bf16[1,2,1,128,128]{4,3,2,1,0:T(8,128)(2,1)S(1)} %get-tuple-element.25), channel_id=1, source_target_pairs={{1,0},{2,1},{3,2},{4,3},{5,4},{6,5},{7,6},{8,7},{9,8},{10,9},{11,1... | collective-permute-start | bytes 196616 | tf_op jit(solution)/shard_map/ppermute | solution.py:31
where the time goes:
time: 322 us; the launch traced here: 321 us
  Pallas kernels  177 us (55%)
  blocking collectives  61.2 us (19%)
  waiting for transfers between devices  48 us (15%)
  starting transfers between devices  15.4 us (5%)
  local copies, waits for them, and re-layouts  11.9 us (4%)
  other arithmetic  3.79 us (1%)
    all_to_all x2, blocking collectives, swap(): lax.all_to_all(sent.reshape(count, planes, sends), 'space', split_axis=0,...  61.2 us
    pallas_call x1, Pallas kernels, local_fast(): pl.pallas_call(lambda *refs: final_kernel(planes, count, *refs), grid=(pl...  54.4 us
    pallas_call x1, Pallas kernels, local_fast(): pl.pallas_call(lambda *refs: lift_kernel(planes, count, *refs), grid=(pla...  52.1 us
    all_to_all x2, waiting for transfers between devices, swap(): lax.all_to_all(sent.reshape(count, planes, sends), 'space', split_axis=0,...  44.9 us
    pallas_call x1, Pallas kernels, local_fast(): pl.pallas_call(lambda *refs: middle_kernel(planes, count, *refs), grid=(p...  44.5 us
    pallas_call x2, Pallas kernels, local_fast(): pl.pallas_call(lambda *refs: mix_kernel(own, *refs), grid=(modes // MODE_...  26.2 us
    all_to_all x2, starting transfers between devices, swap(): lax.all_to_all(sent.reshape(count, planes, sends), 'space', split_axis=0,...  9.82 us
  transfers between devices with their start and end apart: 4, of which 3 were waited for; matrix products, arithmetic and copies ran while one was open for 2% of the time, Pallas kernels for 0%

commit v1 on v0

--- a/solution.py
+++ b/solution.py
@@ -238,6 +238,12 @@
     return np.stack([np.stack([cosine, sine], 1), np.stack([-sine, cosine], 1)], 1)
 
 
+def by_plane(table, axis, count):
+    planes = NX // count
+    order = np.arange(NX).reshape(count, planes).T.reshape(-1)
+    return np.take(table, order, axis)
+
+
 def tables_for(count):
     own = MY // count
     cosine, sine = np_waves(NZ, MZ, True)
@@ -252,8 +258,8 @@
         "zi": np.kron(pair, z_inverse),
         "yf": y_forward.transpose(3, 5, 4, 1, 2, 0).reshape(2 * MY, 2 * NY),
         "yi": y_inverse.transpose(5, 3, 4, 2, 1, 0).reshape(2 * NY, 2 * MY),
-        "xf": np_forward(NX, MX).transpose(1, 2, 3, 0).reshape(2, 2 * MX, NX),
-        "xi": np_inverse(NX, MX).transpose(2, 3, 0, 1).reshape(2, NX, 2 * MX),
+        "xf": by_plane(np_forward(NX, MX).transpose(1, 2, 3, 0).reshape(2, 2 * MX, NX), 2, count),
+        "xi": by_plane(np_inverse(NX, MX).transpose(2, 3, 0, 1).reshape(2, NX, 2 * MX), 1, count),
     }
     return {name: jnp.asarray(table.astype(np.float32)).astype(BF) for name, table in tables.items()}
 
@@ -290,24 +296,39 @@
     return c0, c1, c2, c3
 
 
-def to_modes(plane, planes, count, yf_ref, zs, send, out_ref):
+def send_plane(me, count, plane, send, recv, send_sem, recv_sem):
+    for shift in range(1, count):
+        target = lax.rem(me + shift, count)
+        pltpu.make_async_remote_copy(
+            src_ref=send.at[plane, target],
+            dst_ref=recv.at[plane, me],
+            send_sem=send_sem.at[plane],
+            recv_sem=recv_sem.at[plane],
+            device_id={"space": target},
+            device_id_type=pl.DeviceIdType.MESH,
+        ).start()
+    recv[plane, me] = send[plane, me]
+
+
+def wait_plane(count, plane, buffer, sem):
+    part = buffer.at[plane, pl.ds(0, count - 1)]
+    pltpu.make_async_copy(part, part, sem.at[plane]).wait()
+
+
+def to_modes(plane, count, yf_ref, zs, flat, send):
     pieces = []
     for group in range(C // 4):
         four = [zs[(group * 4 + r) * PITCH : (group * 4 + r) * PITCH + PAIRS, :] for r in range(4)]
         pieces.append(jnp.concatenate([p.astype(BF) for p in swap_blocks(four)], 0))
-    stacked = jnp.concatenate(pieces, 1)
-    modes = dot32(yf_ref[...], stacked)
+    modes = dot32(yf_ref[...], jnp.concatenate(pieces, 1))
     tiles = C * MZ // LANES
+    slots = 2 * MY // count * tiles
     for s in range(2 * MY // count):
         for t in range(tiles):
-            send[s * tiles + t, pl.ds(plane, count, stride=planes), :] = modes[
+            flat[pl.ds(s * tiles + t, count, stride=slots), :] = modes[
                 s * count : (s + 1) * count, t * LANES : (t + 1) * LANES
             ]
-
-    @pl.when(plane == planes - 1)
-    def _():
-        for t in range(send.shape[0]):
-            out_ref[:, t * LANES : (t + 1) * LANES] = send[t].astype(BF)
+    send[plane] = flat[: count * slots, :].reshape(count, slots, LANES).astype(BF)
 
 
 def lay_out(zs, start, values):
@@ -315,17 +336,13 @@
         zs[pl.ds(start + r, C, stride=PITCH), :] = values[r * C : (r + 1) * C, :]
 
 
-def lift_kernel(
-    planes, count, feat_ref, perm_ref, in_ref, lo_ref, zf_ref, yf_ref, hid_ref, out_ref, plain, xs, zs, send
-):
-    plane = pl.program_id(0)
-
-    @pl.when(plane == 0)
-    def _():
-        xs[...] = jnp.zeros_like(xs)
-
+def hid_rows(index):
+    return pl.ds(pl.multiple_of(index * ROWS * C, ROWS * C), ROWS * C)
+
+
+def lift_plane(plane, feat_ref, perm_ref, in_ref, lo_ref, zf_ref, hid, plain, xs, zs):
     for f in range(FIN + 1):
-        plain[...] = perm_ref[0, 0] if f == FIN else feat_ref[0, f, 0].astype(F32)
+        plain[...] = perm_ref[0, plane] if f == FIN else feat_ref[0, f, plane].astype(F32)
         for y2 in range(2):
             xs[y2, pl.ds(f, PAIRS, stride=8), :] = plain[pl.ds(y2, PAIRS, stride=2), :]
     width = lo_ref.shape[1]
@@ -339,26 +356,22 @@
             for r in range(lifted.shape[0] // width)
         ]
         hidden = jnp.concatenate(parts, 0)
-        hid_ref[0, pl.ds(pl.multiple_of(index * ROWS * C, ROWS * C), ROWS * C), :] = hidden
+        hid[plane, hid_rows(index), :] = hidden
         lay_out(zs, index * ROWS, dot32(hidden, zf_ref[...]))
         return carry
 
     lax.fori_loop(0, PAIRS // ROWS, block, 0)
-    to_modes(plane, planes, count, yf_ref, zs, send, out_ref)
-
-
-def from_modes(plane, planes, count, got_ref, yi_ref, recv, zs):
-    @pl.when(plane == 0)
-    def _():
-        for t in range(recv.shape[0]):
-            recv[t] = got_ref[:, t * LANES : (t + 1) * LANES].astype(F32)
-
+
+
+def from_modes(plane, count, recv, yi_ref, flat, zs):
     tiles = C * MZ // LANES
+    slots = 2 * MY // count * tiles
+    flat[: count * slots, :] = recv[plane].astype(F32).reshape(count * slots, LANES)
     rows = []
     for s in range(2 * MY // count):
         rows.append(
             jnp.concatenate(
-                [recv[s * tiles + t, pl.ds(plane, count, stride=planes), :] for t in range(tiles)], 1
+                [flat[pl.ds(s * tiles + t, count, stride=slots), :] for t in range(tiles)], 1
             ).astype(BF)
         )
     back = dot32(yi_ref[...], jnp.concatenate(rows, 0))
@@ -369,101 +382,167 @@
             zs[(group * 4 + r) * PITCH : (group * 4 + r) * PITCH + PAIRS, :] = piece
 
 
-def layer_rows(index, zs, hid_ref, zi_ref, kp_ref):
+def layer_rows(plane, index, zs, hid, zi_ref, kp):
     start = index * ROWS
     parts = [zs[pl.ds(start + r, C, stride=PITCH), :].astype(BF) for r in range(ROWS)]
     spectral = dot32(jnp.concatenate(parts, 0), zi_ref[...])
-    old = hid_ref[0, pl.ds(pl.multiple_of(index * ROWS * C, ROWS * C), ROWS * C), :]
-    return gelu_fast(spectral + dot32(kp_ref[...], old))
-
-
-def middle_kernel(
-    planes, count, got_ref, hid_ref, kp_ref, yi_ref, zi_ref, zf_ref, yf_ref, new_ref, out_ref, recv, zs, zs2, send
-):
-    plane = pl.program_id(0)
-    from_modes(plane, planes, count, got_ref, yi_ref, recv, zs)
-
+    return gelu_fast(spectral + dot32(kp, hid[plane, hid_rows(index), :]))
+
+
+def middle_plane(plane, kp, zi_ref, zf_ref, hid, zs, zs2):
     def block(index, carry):
-        hidden = layer_rows(index, zs, hid_ref, zi_ref, kp_ref)
-        new_ref[0, pl.ds(pl.multiple_of(index * ROWS * C, ROWS * C), ROWS * C), :] = hidden
+        hidden = layer_rows(plane, index, zs, hid, zi_ref, kp)
+        hid[plane, hid_rows(index), :] = hidden
         lay_out(zs2, index * ROWS, dot32(hidden, zf_ref[...]))
         return carry
 
     lax.fori_loop(0, PAIRS // ROWS, block, 0)
-    to_modes(plane, planes, count, yf_ref, zs2, send, out_ref)
-
-
-def final_kernel(
-    planes, count, got_ref, hid_ref, kp_ref, yi_ref, zi_ref, di_ref, do_ref, perm_ref, st_ref, cond_ref, recv, zs
-):
-    plane = pl.program_id(0)
-    from_modes(plane, planes, count, got_ref, yi_ref, recv, zs)
-
+
+
+def final_plane(plane, kp, zi_ref, di_ref, do_ref, perm_ref, hid, zs, st_ref, cond_ref):
     def block(index, carry):
-        hidden = layer_rows(index, zs, hid_ref, zi_ref, kp_ref)
-        decoded = gelu_fast(dot32(di_ref[...], hidden))
-        both = dot32(do_ref[...], decoded)
+        hidden = layer_rows(plane, index, zs, hid, zi_ref, kp)
+        both = dot32(do_ref[...], gelu_fast(dot32(di_ref[...], hidden)))
         for y2 in range(2):
             lanes = slice(y2 * NZ, (y2 + 1) * NZ)
             where = pl.ds(index * ROWS * 2 + y2, ROWS, stride=2)
-            st_ref[0, 0, 0, where, :] = both[:ROWS, lanes]
-            st_ref[0, 1, 0, where, :] = both[ROWS:, lanes]
+            st_ref[0, 0, plane, where, :] = both[:ROWS, lanes]
+            st_ref[0, 1, plane, where, :] = both[ROWS:, lanes]
         return carry
 
     lax.fori_loop(0, PAIRS // ROWS, block, 0)
-    sat = jax.nn.sigmoid(st_ref[0, 1, 0])
-    st_ref[0, 1, 0] = sat
-    cond_ref[0, 0] = mobility_of(sat, perm_ref[0, 0])
-
-
-def mix_kernel(own, a_ref, w_ref, xf_ref, xi_ref, out_ref, spec, mixed, turned, rhs):
-    step = pl.program_id(0)
-    half = C * own * MZ
+    sat = jax.nn.sigmoid(st_ref[0, 1, plane])
+    st_ref[0, 1, plane] = sat
+    cond_ref[0, plane] = mobility_of(sat, perm_ref[0, plane])
+
+
+def mix_modes(planes, count, recv, send, wbuf, xf_ref, xi_ref, flat, spec, mixed, turned, rhs):
+    own = MY // count
+    tiles = C * MZ // LANES
+    slots = 2 * own * tiles
+    every = count * planes
     wide = MX * 2 * C
-
-    @pl.when(step == 0)
-    def _():
-        total = dot32(xf_ref[0], a_ref[:, :half]) + dot32(xf_ref[1], a_ref[:, half:])
-        spec[:, : 2 * MX] = total.T
-
-    first = step * MODE_STEP
-    base = first // MZ * (C * MZ) + first % MZ
-    rows = [spec[pl.ds(base + r, C, stride=MZ), :] for r in range(MODE_STEP)]
-    values = jnp.concatenate(rows, 0)[:, : 2 * MX].astype(BF)
+    for plane in range(planes):
+        flat[plane * count * slots : (plane + 1) * count * slots, :] = (
+            recv[plane].astype(F32).reshape(count * slots, LANES)
+        )
+    total = 0.0
+    for p in range(2):
+        right = jnp.concatenate(
+            [
+                flat[pl.ds(p * own * tiles + t, every, stride=slots), :].astype(BF)
+                for t in range(own * tiles)
+            ],
+            1,
+        )
+        total = total + dot32(xf_ref[p], right)
+    spec[:, : 2 * MX] = total.T
     chunk = 512
-    for piece in range(wide // chunk):
-        lo = piece * chunk
-        row = lax.broadcasted_iota(jnp.int32, (2 * MX, chunk), 0)
-        col = lax.broadcasted_iota(jnp.int32, (2 * MX, chunk), 1) + lo
-        weights = w_ref[0, :, :, lo : lo + chunk].reshape(MODE_STEP * C, chunk).astype(F32)
-        sums = []
-        for q in range(2):
-            pick = jnp.where(row == col // (2 * C) + q * MX, 1.0, 0.0).astype(BF)
-            terms = dot32(values, pick) * weights
-            sums.append(jnp.sum(terms.reshape(MODE_STEP, C, chunk), 1))
-        lane = lax.broadcasted_iota(jnp.int32, (MODE_STEP, chunk), 1)
-        turn = jnp.where(
-            lane % (2 * C) < C, -pltpu.roll(sums[1], chunk - C, 1), pltpu.roll(sums[1], C, 1)
-        )
-        mixed[pl.ds(pl.multiple_of(first, MODE_STEP), MODE_STEP), lo : lo + chunk] = sums[0] + turn
-
-    @pl.when(step == pl.num_programs(0) - 1)
-    def _():
-        modes = own * MZ
-        turned[:, :modes] = mixed[...].T
-        for o in range(C):
-            piece = turned[pl.ds(o, 2 * MX, stride=C), :]
-            for jj in range(own):
-                lo = (jj * C + o) * MZ
-                rhs[:, lo : lo + MZ] = piece[:, jj * MZ : (jj + 1) * MZ]
-        right = rhs[...].astype(BF)
-        for p in range(2):
-            out_ref[:, p * half : (p + 1) * half] = dot32(xi_ref[p], right).astype(BF)
-
-
-def whole_spec(array):
-    dims = array.ndim
-    return pl.BlockSpec(array.shape, lambda i: (0,) * dims)
+
+    def step(index, carry):
+        first = pl.multiple_of(index * MODE_STEP, MODE_STEP)
+        base = first // MZ * (C * MZ) + first % MZ
+        rows = [spec[pl.ds(base + r, C, stride=MZ), :] for r in range(MODE_STEP)]
+        values = jnp.concatenate(rows, 0)[:, : 2 * MX].astype(BF)
+        for piece in range(wide // chunk):
+            lo = piece * chunk
+            row = lax.broadcasted_iota(jnp.int32, (2 * MX, chunk), 0)
+            col = lax.broadcasted_iota(jnp.int32, (2 * MX, chunk), 1) + lo
+            weights = wbuf[pl.ds(first, MODE_STEP), :, lo : lo + chunk]
+            weights = weights.reshape(MODE_STEP * C, chunk).astype(F32)
+            sums = []
+            for q in range(2):
+                pick = jnp.where(row == col // (2 * C) + q * MX, 1.0, 0.0).astype(BF)
+                terms = dot32(values, pick) * weights
+                sums.append(jnp.sum(terms.reshape(MODE_STEP, C, chunk), 1))
+            lane = lax.broadcasted_iota(jnp.int32, (MODE_STEP, chunk), 1)
+            turn = jnp.where(
+                lane % (2 * C) < C, -pltpu.roll(sums[1], chunk - C, 1), pltpu.roll(sums[1], C, 1)
+            )
+            mixed[pl.ds(first, MODE_STEP), lo : lo + chunk] = sums[0] + turn
+        return carry
+
+    lax.fori_loop(0, own * MZ // MODE_STEP, step, 0)
+    turned[:, : own * MZ] = mixed[...].T
+    for o in range(C):
+        piece = turned[pl.ds(o, 2 * MX, stride=C), :]
+        for jj in range(own):
+            lo = (jj * C + o) * MZ
+            rhs[:, lo : lo + MZ] = piece[:, jj * MZ : (jj + 1) * MZ]
+    right = rhs[...].astype(BF)
+    for p in range(2):
+        back = dot32(xi_ref[p], right)
+        for t in range(own * tiles):
+            flat[pl.ds(p * own * tiles + t, every, stride=slots), :] = back[
+                :, t * LANES : (t + 1) * LANES
+            ]
+    for plane in range(planes):
+        send[plane] = (
+            flat[plane * count * slots : (plane + 1) * count * slots, :]
+            .reshape(count, slots, LANES)
+            .astype(BF)
+        )
+
+
+def whole_kernel(
+    planes, count, feat_ref, perm_ref, in_ref, lo_ref, kp_ref, di_ref, do_ref, zf_ref, zi_ref,
+    yf_ref, yi_ref, xf_ref, xi_ref, w_hbm, st_ref, cond_ref,
+    hid, wbuf, send_f, recv_f, send_b, recv_b, flat, spec, mixed, turned, rhs, zs, zs2, xs, plain,
+    w_sem, sf_sem, rf_sem, sb_sem, rb_sem,
+):
+    me = lax.axis_index("space")
+    barrier = pltpu.get_barrier_semaphore()
+    for shift in range(1, count):
+        pl.semaphore_signal(
+            barrier,
+            inc=1,
+            device_id={"space": lax.rem(me + shift, count)},
+            device_id_type=pl.DeviceIdType.MESH,
+        )
+    fetch = pltpu.make_async_copy(w_hbm.at[0], wbuf, w_sem.at[0])
+    fetch.start()
+    xs[...] = jnp.zeros_like(xs)
+    pl.semaphore_wait(barrier, count - 1)
+
+    def over(body):
+        def run(plane, carry):
+            body(plane)
+            return carry
+
+        lax.fori_loop(0, planes, run, 0)
+
+    def lift(plane):
+        lift_plane(plane, feat_ref, perm_ref, in_ref, lo_ref, zf_ref, hid, plain, xs, zs)
+        to_modes(plane, count, yf_ref, zs, flat, send_f)
+        send_plane(me, count, plane, send_f, recv_f, sf_sem, rf_sem)
+
+    over(lift)
+    for layer in range(LAYERS):
+        fetch.wait()
+        over(lambda plane: wait_plane(count, plane, recv_f, rf_sem))
+        over(lambda plane: wait_plane(count, plane, send_f, sf_sem))
+        mix_modes(
+            planes, count, recv_f, send_b, wbuf, xf_ref, xi_ref, flat, spec, mixed, turned, rhs
+        )
+        if layer + 1 < LAYERS:
+            fetch = pltpu.make_async_copy(w_hbm.at[layer + 1], wbuf, w_sem.at[layer + 1])
+            fetch.start()
+        over(lambda plane: send_plane(me, count, plane, send_b, recv_b, sb_sem, rb_sem))
+
+        def rest(plane):
+            wait_plane(count, plane, recv_b, rb_sem)
+            from_modes(plane, count, recv_b, yi_ref, flat, zs)
+            if layer + 1 < LAYERS:
+                middle_plane(plane, kp_ref[layer], zi_ref, zf_ref, hid, zs, zs2)
+                to_modes(plane, count, yf_ref, zs2, flat, send_f)
+                send_plane(me, count, plane, send_f, recv_f, sf_sem, rf_sem)
+            else:
+                final_plane(
+                    plane, kp_ref[layer], zi_ref, di_ref, do_ref, perm_ref, hid, zs, st_ref, cond_ref
+                )
+
+        over(rest)
+        over(lambda plane: wait_plane(count, plane, send_b, sb_sem))
 
 
 def block_diag(matrix, copies):
@@ -487,103 +566,56 @@
     planes = features.shape[2]
     count = lax.axis_size("space")
     own = MY // count
+    modes = own * MZ
+    slots = 2 * modes * C // LANES
     tables = tables_for(count)
-    params = pltpu.CompilerParams(
-        dimension_semantics=("arbitrary",), vmem_limit_bytes=56 * 1024 * 1024
-    )
-    sends = 2 * own * C * MZ
-    tiles = sends // LANES
-    hid_shape = jax.ShapeDtypeStruct((planes, PAIRS * C, 2 * NZ), BF)
-    send_shape = jax.ShapeDtypeStruct((count * planes, sends), BF)
-    hid_spec = pl.BlockSpec((1, PAIRS * C, 2 * NZ), lambda i: (i, 0, 0))
-    send_spec = pl.BlockSpec((count * planes, sends), lambda i: (0, 0))
-    zs_scratch = pltpu.VMEM((C * PITCH, LANES), F32)
-    send_scratch = pltpu.VMEM((tiles, count * planes, LANES), F32)
-    perm_spec = pl.BlockSpec((1, 1, NY, NZ), lambda i: (0, i, 0, 0))
-    in_rows = jnp.pad(lift_in, ((0, 8 - FIN - 1), (0, 0))).T
-    k_in = block_diag(in_rows, ROWS)
-    k_lo = block_diag(lift_out.T, 2)
-    k_di = block_diag(dec_in.T, ROWS)
+    in_rows = jnp.pad(lift_in, ((0, 0 + 8 - FIN - 1), (0, 0))).T
+    k_p = jnp.stack([block_diag(point_weight[layer].T, ROWS) for layer in range(LAYERS)])
     eye = jnp.eye(ROWS, dtype=BF)
     k_do = (dec_out.T[:, None, None, :] * eye[None, :, :, None]).reshape(2 * ROWS, -1)
-
-    def swap(sent):
-        return lax.all_to_all(
-            sent.reshape(count, planes, sends), "space", split_axis=0, concat_axis=0, tiled=True
-        ).reshape(count * planes, sends)
-
-    operands = (features, log_perm, k_in, k_lo, tables["zf"], tables["yf"])
-    hidden, sent = pl.pallas_call(
-        lambda *refs: lift_kernel(planes, count, *refs),
-        grid=(planes,),
-        in_specs=[pl.BlockSpec((1, FIN, 1, NY, NZ), lambda i: (0, 0, i, 0, 0)), perm_spec]
-        + [whole_spec(a) for a in operands[2:]],
-        out_specs=[hid_spec, send_spec],
-        out_shape=[hid_shape, send_shape],
+    operands = (
+        features,
+        log_perm,
+        block_diag(in_rows, ROWS),
+        block_diag(lift_out.T, 2),
+        k_p,
+        block_diag(dec_in.T, ROWS),
+        k_do,
+    ) + tuple(tables[name] for name in ("zf", "zi", "yf", "yi", "xf", "xi"))
+    vmem = pl.BlockSpec(memory_space=pltpu.VMEM)
+    exchange = pltpu.VMEM((planes, count, slots, LANES), BF)
+    states, conduct = pl.pallas_call(
+        lambda *refs: whole_kernel(planes, count, *refs),
+        in_specs=[vmem] * len(operands) + [pl.BlockSpec(memory_space=pl.ANY)],
+        out_specs=[vmem, vmem],
+        out_shape=[
+            jax.ShapeDtypeStruct((1, 2, planes, NY, NZ), F32),
+            jax.ShapeDtypeStruct((1, planes, NY, NZ), F32),
+        ],
         scratch_shapes=[
+            pltpu.VMEM((planes, PAIRS * C, 2 * NZ), BF),
+            pltpu.VMEM(spec_weight.shape[1:], BF),
+            exchange,
+            exchange,
+            exchange,
+            exchange,
+            pltpu.VMEM((planes * count * slots, LANES), F32),
+            pltpu.VMEM((modes * C, LANES), F32),
+            pltpu.VMEM((modes, MX * 2 * C), F32),
+            pltpu.VMEM((MX * 2 * C, LANES), F32),
+            pltpu.VMEM((2 * MX, modes * C), F32),
+            pltpu.VMEM((C * PITCH, LANES), F32),
+            pltpu.VMEM((C * PITCH, LANES), F32),
+            pltpu.VMEM((2, PAIRS * 8, NZ), F32),
             pltpu.VMEM((NY, NZ), F32),
-            pltpu.VMEM((2, PAIRS * 8, NZ), F32),
-            zs_scratch,
-            send_scratch,
-        ],
-        compiler_params=params,
-        name="lift",
-    )(*operands)
-    for layer_idx in range(LAYERS):
-        arrived = swap(sent)
-        modes = own * MZ
-        mixed = pl.pallas_call(
-            lambda *refs: mix_kernel(own, *refs),
-            grid=(modes // MODE_STEP,),
-            in_specs=[
-                send_spec,
-                pl.BlockSpec(
-                    (1, MODE_STEP, C, MX * 2 * C), lambda i, layer=layer_idx: (layer, i, 0, 0)
-                ),
-                whole_spec(tables["xf"]),
-                whole_spec(tables["xi"]),
-            ],
-            out_specs=send_spec,
-            out_shape=send_shape,
-            scratch_shapes=[
-                pltpu.VMEM((modes * C, LANES), F32),
-                pltpu.VMEM((modes, MX * 2 * C), F32),
-                pltpu.VMEM((MX * 2 * C, LANES), F32),
-                pltpu.VMEM((2 * MX, modes * C), F32),
-            ],
-            compiler_params=params,
-            name="mix",
-        )(arrived, spec_weight, tables["xf"], tables["xi"])
-        returned = swap(mixed)
-        k_p = block_diag(point_weight[layer_idx].T, ROWS)
-        shared = (returned, hidden, k_p, tables["yi"], tables["zi"])
-        shared_specs = [send_spec, hid_spec] + [whole_spec(a) for a in shared[2:]]
-        if layer_idx < LAYERS - 1:
-            operands = shared + (tables["zf"], tables["yf"])
-            hidden, sent = pl.pallas_call(
-                lambda *refs: middle_kernel(planes, count, *refs),
-                grid=(planes,),
-                in_specs=shared_specs + [whole_spec(a) for a in operands[5:]],
-                out_specs=[hid_spec, send_spec],
-                out_shape=[hid_shape, send_shape],
-                scratch_shapes=[send_scratch, zs_scratch, zs_scratch, send_scratch],
-                compiler_params=params,
-                name="middle",
-            )(*operands)
-        else:
-            states, conduct = pl.pallas_call(
-                lambda *refs: final_kernel(planes, count, *refs),
-                grid=(planes,),
-                in_specs=shared_specs + [whole_spec(k_di), whole_spec(k_do), perm_spec],
-                out_specs=[pl.BlockSpec((1, 2, 1, NY, NZ), lambda i: (0, 0, i, 0, 0)), perm_spec],
-                out_shape=[
-                    jax.ShapeDtypeStruct((1, 2, planes, NY, NZ), F32),
-                    jax.ShapeDtypeStruct((1, planes, NY, NZ), F32),
-                ],
-                scratch_shapes=[send_scratch, zs_scratch],
-                compiler_params=params,
-                name="final",
-            )(*shared, k_di, k_do, log_perm)
+            pltpu.SemaphoreType.DMA((LAYERS,)),
+        ]
+        + [pltpu.SemaphoreType.DMA((planes,))] * 4,
+        compiler_params=pltpu.CompilerParams(
+            collective_id=0, has_side_effects=True, vmem_limit_bytes=60 * 1024 * 1024
+        ),
+        name="whole",
+    )(*operands, spec_weight)
     return (states, darcy(states[:, 0], conduct, well_cells, well_rates))
 
 

time: 322 us -> 221 us (0.69)
  blocking collectives: 61.2 us -> 0 us
  waiting for transfers between devices: 48 us -> 2.94 us
  Pallas kernels: 177 us -> 197 us
  starting transfers between devices: 15.4 us -> 4.33 us
  local copies, waits for them, and re-layouts: 11.9 us -> 8.59 us
    all_to_all x2 -> x0, blocking collectives: 61.2 us -> none  [swap(): lax.all_to_all(sent.reshape(count, planes, sends), 'space', split_axis=0,...]
    all_to_all x2 -> x0, waiting for transfers between devices: 44.9 us -> none  [swap(): lax.all_to_all(sent.reshape(count, planes, sends), 'space', split_axis=0,...]
    pallas_call x5 -> x1, Pallas kernels: 177 us -> 197 us  [local_fast(): pl.pallas_call(lambda *refs: whole_kernel(planes, count, *refs), in_specs...]
    all_to_all x2 -> x0, starting transfers between devices: 9.82 us -> none  [swap(): lax.all_to_all(sent.reshape(count, planes, sends), 'space', split_axis=0,...]
  transfers between devices with their start and end apart: 4 -> 2, of which waited for: 3 -> 1; matrix products, arithmetic and copies ran while one was open for 2% -> 0% of each run, Pallas kernels for 0% -> 0%
where the time goes in v1:
time: 221 us
  Pallas kernels  197 us (89%)
  local copies, waits for them, and re-layouts  8.59 us (4%)
  other arithmetic  4.82 us (2%)
  starting transfers between devices  4.33 us (2%)
  waiting for transfers between devices  2.94 us (1%)
  matrix products  2.38 us (1%)
    pallas_call x1, Pallas kernels, local_fast(): pl.pallas_call(lambda *refs: whole_kernel(planes, count, *refs), in_specs...  197 us
  transfers between devices with their start and end apart: 2, of which 1 were waited for; matrix products, arithmetic and copies ran while one was open for 0% of the time, Pallas kernels for 0%

profile of v1, /device:TPU:13, one launch (start us, length us, event | category | flops | bytes accessed | tf_op | source)
XLA Modules:
  0.0 220.7 jit_solution(14050989392132302160)
XLA Ops:
  0.7 0.7 pad_bitcast_fusion
  1.4 0.7 slice_bitcast_fusion.2
  2.3 0.8 broadcast_multiply_fusion.5
  3.1 0.6 copy.43
  3.7 0.7 broadcast_multiply_fusion.4
  4.5 0.7 mul.213.refs_6_
  5.3 0.8 copy.26.refs_2_
  6.1 0.8 broadcast_multiply_fusion
  6.9 0.3 mul.209
  7.2 0.8 copy.27.refs_5_
  8.1 0.1 broadcast_multiply_fusion.2
  8.2 0.4 mul.202
  8.6 0.4 mul.205
  8.9 0.7 pad_maximum_fusion.2.refs_4_
  9.7 196.8 %whole.1 = (f32[1,2,8,128,128]{4,3,2,1,0:T(8,128)}, f32[1,8,128,128]{3,2,1,0:T(8,128)}) custom-call(bf16[1,4,8,128,128]{4,3,2,1,0:T(8,128)(2,1)} %refs_0_.1, f32[1,8,128,128]{3,2,1,0:T(8,128)} %refs_1_.1, bf16[1024,64]{1,0:T(8,128)(2,1)} %copy.26.refs_2_, bf16[64,256]{1,0:T(8,128)(2,1)} %bitcast.82, bf16[2,256,256]{2,1,0:T(8,128)(2,1)} %pad_maximum_fusion.2.refs_4_, ...), custom_call_target="tpu_custom_call" | custom-call | tf_op jit(solution)/shard_map/whole/pallas_call | solution.py:587
  206.5 1.1 convert_bitcast_fusion.4
  207.6 1.2 fusion.31
  208.9 1.9 collective-permute-start
  210.8 2.4 %collective-permute-start.1 = (bf16[1,2,1,128,128]{4,3,2,1,0:T(8,128)(2,1)S(1)}, bf16[1,2,1,128,128]{4,3,2,1,0:T(8,128)(2,1)S(1)}, u32[]{:S(2)}, u32[]{:S(2)}) collective-permute-start(bf16[1,2,1,128,128]{4,3,2,1,0:T(8,128)(2,1)S(1)} %get-tuple-element.17), channel_id=1, source_target_pairs={{1,0},{2,1},{3,2},{4,3},{5,4},{6,5},{7,6},{8,7},{9,8},{10,9},{11,1... | collective-permute-start | bytes 196616 | tf_op jit(solution)/shard_map/ppermute | solution.py:31
  213.5 0.2 fusion.32
  213.7 0.5 copy-done.3
  214.4 2.9 %collective-permute-done.1 = bf16[1,2,1,128,128]{4,3,2,1,0:T(8,128)(2,1)S(1)} collective-permute-done((bf16[1,2,1,128,128]{4,3,2,1,0:T(8,128)(2,1)S(1)}, bf16[1,2,1,128,128]{4,3,2,1,0:T(8,128)(2,1)S(1)}, u32[]{:S(2)}, u32[]{:S(2)}) %collective-permute-start.1) | collective-permute-done | bytes 65568 | tf_op jit(solution)/shard_map/ppermute | solution.py:31
  217.3 2.4 %fusion = f32[1,8,128,128]{3,2,1,0:T(8,128)} fusion(f32[1,8,128,128]{3,2,1,0:T(8,128)S(1)} %slice_bitcast_fusion, f32[1,7,128,128]{3,2,1,0:T(8,128)S(1)} %get-tuple-element.25, f32[1,1,128,128]{3,2,1,0:T(8,128)S(1)} %get-tuple-element.10, f32[1,1,128,128]{3,2,1,0:T(8,128)S(1)} %get-tuple-element.11, f32[1,7,128,128]{3,2,1,0:T(8,128)S(1)} %get-tuple-element.26, ...), kind=kOutput, calls=%fused_computation.9 | convolution fusion | flops 55709696 | bytes 3801216 | tf_op jit(solution)/shard_map/bwa,bwz->baz/dot_general | solution.py:133
  219.7 1.0 copy.45
  (24 shorter events, 0.8 us)
Async XLA Ops:
  206.5 6.8 %copy-start = (f32[1,8,128,128]{3,2,1,0:T(8,128)S(1)}, f32[1,8,128,128]{3,2,1,0:T(8,128)}, u32[]{:S(2)}) copy-start(f32[1,8,128,128]{3,2,1,0:T(8,128)} %get-tuple-element.5) | copy-start | bytes 1572868
  207.6 5.7 %copy-start.1 = (f32[1,2,8,128,128]{4,3,2,1,0:T(8,128)S(1)}, f32[1,2,8,128,128]{4,3,2,1,0:T(8,128)}, u32[]{:S(2)}) copy-start(f32[1,2,8,128,128]{4,3,2,1,0:T(8,128)} %get-tuple-element.29) | copy-start | bytes 3145732
  208.9 4.5 %copy-start.2 = (s32[1,32]{1,0:T(1,128)S(1)}, s32[1,32]{1,0:T(1,128)}, u32[]{:S(2)}) copy-start(s32[1,32]{1,0:T(1,128)} %param.18) | copy-start | bytes 388
  208.9 5.5 %collective-permute-start = (bf16[1,2,1,128,128]{4,3,2,1,0:T(8,128)(2,1)S(1)}, bf16[1,2,1,128,128]{4,3,2,1,0:T(8,128)(2,1)S(1)}, u32[]{:S(2)}, u32[]{:S(2)}) collective-permute-start(bf16[1,2,1,128,128]{4,3,2,1,0:T(8,128)(2,1)S(1)} %get-tuple-element.16), channel_id=1, source_target_pairs={{0,1},{1,2},{2,3},{3,4},{4,5},{5,6},{6,7},{7,8},{8,9},{9,10},{10,1... | collective-permute-start | bytes 196616 | tf_op jit(solution)/shard_map/ppermute | solution.py:28
  210.8 6.5 %collective-permute-start.1 = (bf16[1,2,1,128,128]{4,3,2,1,0:T(8,128)(2,1)S(1)}, bf16[1,2,1,128,128]{4,3,2,1,0:T(8,128)(2,1)S(1)}, u32[]{:S(2)}, u32[]{:S(2)}) collective-permute-start(bf16[1,2,1,128,128]{4,3,2,1,0:T(8,128)(2,1)S(1)} %get-tuple-element.17), channel_id=1, source_target_pairs={{1,0},{2,1},{3,2},{4,3},{5,4},{6,5},{7,6},{8,7},{9,8},{10,9},{11,1... | collective-permute-start | bytes 196616 | tf_op jit(solution)/shard_map/ppermute | solution.py:31
  213.5 0.7 copy-start.3

commit v2 on v1

--- a/solution.py
+++ b/solution.py
@@ -217,6 +217,7 @@
 PITCH = PAIRS + 8
 MODE_STEP = 8
 ROWS = 8
+UNROLL = 4
 LANES = 128
 
 
@@ -255,7 +256,7 @@
     pair = np.eye(2)
     tables = {
         "zf": np.kron(pair, z_forward),
-        "zi": np.kron(pair, z_inverse),
+        "zi": 0.5 * np.kron(pair, z_inverse),
         "yf": y_forward.transpose(3, 5, 4, 1, 2, 0).reshape(2 * MY, 2 * NY),
         "yi": y_inverse.transpose(5, 3, 4, 2, 1, 0).reshape(2 * NY, 2 * MY),
         "xf": by_plane(np_forward(NX, MX).transpose(1, 2, 3, 0).reshape(2, 2 * MX, NX), 2, count),
@@ -268,12 +269,11 @@
     return jnp.dot(a, b, preferred_element_type=F32)
 
 
-def gelu_fast(values):
-    v = values.astype(BF)
+def gelu_of_half(values):
+    u = values.astype(BF)
     scale = math.sqrt(2.0 / math.pi)
-    inner = v * (BF(scale) + BF(scale * 0.044715) * (v * v))
-    half = BF(0.5) * v
-    return half + half * jnp.tanh(inner)
+    inner = u * (BF(2.0 * scale) + BF(8.0 * scale * 0.044715) * (u * u))
+    return u + u * jnp.tanh(inner)
 
 
 def swap_blocks(four):
@@ -350,7 +350,7 @@
     def block(index, carry):
         start = pl.multiple_of(index * ROWS * 8, ROWS * 8)
         x = jnp.concatenate([xs[0, pl.ds(start, ROWS * 8), :], xs[1, pl.ds(start, ROWS * 8), :]], 1)
-        lifted = gelu_fast(dot32(in_ref[...], x.astype(BF)))
+        lifted = gelu_of_half(dot32(in_ref[...], x.astype(BF)))
         parts = [
             dot32(lo_ref[...], lifted[r * width : (r + 1) * width, :]).astype(BF)
             for r in range(lifted.shape[0] // width)
@@ -360,7 +360,7 @@
         lay_out(zs, index * ROWS, dot32(hidden, zf_ref[...]))
         return carry
 
-    lax.fori_loop(0, PAIRS // ROWS, block, 0)
+    lax.fori_loop(0, PAIRS // ROWS, block, 0, unroll=UNROLL)
 
 
 def from_modes(plane, count, recv, yi_ref, flat, zs):
@@ -386,7 +386,7 @@
     start = index * ROWS
     parts = [zs[pl.ds(start + r, C, stride=PITCH), :].astype(BF) for r in range(ROWS)]
     spectral = dot32(jnp.concatenate(parts, 0), zi_ref[...])
-    return gelu_fast(spectral + dot32(kp, hid[plane, hid_rows(index), :]))
+    return gelu_of_half(spectral + dot32(kp, hid[plane, hid_rows(index), :]))
 
 
 def middle_plane(plane, kp, zi_ref, zf_ref, hid, zs, zs2):
@@ -396,13 +396,13 @@
         lay_out(zs2, index * ROWS, dot32(hidden, zf_ref[...]))
         return carry
 
-    lax.fori_loop(0, PAIRS // ROWS, block, 0)
+    lax.fori_loop(0, PAIRS // ROWS, block, 0, unroll=UNROLL)
 
 
 def final_plane(plane, kp, zi_ref, di_ref, do_ref, perm_ref, hid, zs, st_ref, cond_ref):
     def block(index, carry):
         hidden = layer_rows(plane, index, zs, hid, zi_ref, kp)
-        both = dot32(do_ref[...], gelu_fast(dot32(di_ref[...], hidden)))
+        both = dot32(do_ref[...], gelu_of_half(dot32(di_ref[...], hidden)))
         for y2 in range(2):
             lanes = slice(y2 * NZ, (y2 + 1) * NZ)
             where = pl.ds(index * ROWS * 2 + y2, ROWS, stride=2)
@@ -410,7 +410,7 @@
             st_ref[0, 1, plane, where, :] = both[ROWS:, lanes]
         return carry
 
-    lax.fori_loop(0, PAIRS // ROWS, block, 0)
+    lax.fori_loop(0, PAIRS // ROWS, block, 0, unroll=UNROLL)
     sat = jax.nn.sigmoid(st_ref[0, 1, plane])
     st_ref[0, 1, plane] = sat
     cond_ref[0, plane] = mobility_of(sat, perm_ref[0, plane])
@@ -485,10 +485,10 @@
 
 
 def whole_kernel(
-    planes, count, feat_ref, perm_ref, in_ref, lo_ref, kp_ref, di_ref, do_ref, zf_ref, zi_ref,
+    planes, count, feat_ref, perm_ref, lift_in, lift_out, point, dec_in, dec_out, zf_ref, zi_ref,
     yf_ref, yi_ref, xf_ref, xi_ref, w_hbm, st_ref, cond_ref,
     hid, wbuf, send_f, recv_f, send_b, recv_b, flat, spec, mixed, turned, rhs, zs, zs2, xs, plain,
-    w_sem, sf_sem, rf_sem, sb_sem, rb_sem,
+    in_ref, lo_ref, kp_ref, di_ref, do_ref, w_sem, sf_sem, rf_sem, sb_sem, rb_sem,
 ):
     me = lax.axis_index("space")
     barrier = pltpu.get_barrier_semaphore()
@@ -502,6 +502,21 @@
     fetch = pltpu.make_async_copy(w_hbm.at[0], wbuf, w_sem.at[0])
     fetch.start()
     xs[...] = jnp.zeros_like(xs)
+    in_ref[...] = diag_of(lift_in[...], ROWS, 8, 0.5)
+    lo_ref[...] = diag_of(lift_out[...], 2, lift_out.shape[0], 1.0)
+    for layer in range(LAYERS):
+        kp_ref[layer] = diag_of(point[layer], ROWS, C, 0.5)
+    di_ref[...] = diag_of(dec_in[...], ROWS, C, 0.5)
+    dec = dec_out.shape[0]
+    do_ref[...] = spread(
+        dec_out[...],
+        2 * ROWS,
+        ROWS * dec,
+        lambda i: i // ROWS,
+        lambda j: j % dec,
+        lambda i, j: i % ROWS == j // dec,
+        1.0,
+    )
     pl.semaphore_wait(barrier, count - 1)
 
     def over(body):
@@ -545,10 +560,30 @@
         over(lambda plane: wait_plane(count, plane, send_b, sb_sem))
 
 
-def block_diag(matrix, copies):
-    rows, cols = matrix.shape
-    eye = jnp.eye(copies, dtype=matrix.dtype)
-    return (eye[:, None, :, None] * matrix[None, :, None, :]).reshape(copies * rows, copies * cols)
+def ones_where(shape, test, value=1.0):
+    row = lax.broadcasted_iota(jnp.int32, shape, 0)
+    col = lax.broadcasted_iota(jnp.int32, shape, 1)
+    return jnp.where(test(row, col), value, 0.0)
+
+
+def spread(matrix, rows, cols, row_of, col_of, keep, value):
+    take = ones_where((rows, matrix.shape[1]), lambda i, j: row_of(i) == j).astype(BF)
+    put = ones_where((matrix.shape[0], cols), lambda i, j: col_of(j) == i).astype(BF)
+    part = lax.dot_general(take, matrix, (((1,), (1,)), ((), ())), preferred_element_type=F32)
+    return (dot32(part.astype(BF), put) * ones_where((rows, cols), keep, value)).astype(BF)
+
+
+def diag_of(matrix, copies, width, value):
+    depth, height = matrix.shape
+    return spread(
+        matrix,
+        copies * height,
+        copies * width,
+        lambda i: i % height,
+        lambda j: j % width,
+        lambda i, j: i // height == j // width,
+        value,
+    )
 
 
 def local_fast(
@@ -569,18 +604,15 @@
     modes = own * MZ
     slots = 2 * modes * C // LANES
     tables = tables_for(count)
-    in_rows = jnp.pad(lift_in, ((0, 0 + 8 - FIN - 1), (0, 0))).T
-    k_p = jnp.stack([block_diag(point_weight[layer].T, ROWS) for layer in range(LAYERS)])
-    eye = jnp.eye(ROWS, dtype=BF)
-    k_do = (dec_out.T[:, None, None, :] * eye[None, :, :, None]).reshape(2 * ROWS, -1)
+    lift, dec = lift_in.shape[1], dec_in.shape[1]
     operands = (
         features,
         log_perm,
-        block_diag(in_rows, ROWS),
-        block_diag(lift_out.T, 2),
-        k_p,
-        block_diag(dec_in.T, ROWS),
-        k_do,
+        lift_in,
+        lift_out,
+        point_weight,
+        dec_in,
+        dec_out,
     ) + tuple(tables[name] for name in ("zf", "zi", "yf", "yi", "xf", "xi"))
     vmem = pl.BlockSpec(memory_space=pltpu.VMEM)
     exchange = pltpu.VMEM((planes, count, slots, LANES), BF)
@@ -608,6 +640,11 @@
             pltpu.VMEM((C * PITCH, LANES), F32),
             pltpu.VMEM((2, PAIRS * 8, NZ), F32),
             pltpu.VMEM((NY, NZ), F32),
+            pltpu.VMEM((ROWS * lift, ROWS * 8), BF),
+            pltpu.VMEM((2 * C, 2 * lift), BF),
+            pltpu.VMEM((LAYERS, ROWS * C, ROWS * C), BF),
+            pltpu.VMEM((ROWS * dec, ROWS * C), BF),
+            pltpu.VMEM((2 * ROWS, ROWS * dec), BF),
             pltpu.SemaphoreType.DMA((LAYERS,)),
         ]
         + [pltpu.SemaphoreType.DMA((planes,))] * 4,

time: 221 us -> 189 us (0.86)
  Pallas kernels: 197 us -> 171 us
  other arithmetic: 4.82 us -> 1.53 us
  local copies, waits for them, and re-layouts: 8.59 us -> 5.67 us
    pallas_call x1, Pallas kernels: 197 us -> 171 us  [local_fast(): pl.pallas_call(lambda *refs: whole_kernel(planes, count, *refs), in_specs...]
    mul x6 -> x0, local copies, waits for them, and re-layouts: 3.4 us -> none  [the longest x5 2.71 us: block_diag(): eye[:, None, :, None] * matrix[None, :, None, :]]
    mul x4 -> x0, other arithmetic: 2.47 us -> none  [the longest x3 1.74 us: block_diag(): eye[:, None, :, None] * matrix[None, :, None, :]]
where the time goes in v2:
time: 189 us
  Pallas kernels  171 us (90%)
  local copies, waits for them, and re-layouts  5.67 us (3%)
  starting transfers between devices  4.33 us (2%)
  waiting for transfers between devices  2.94 us (2%)
  matrix products  2.38 us (1%)
    pallas_call x1, Pallas kernels, local_fast(): pl.pallas_call(lambda *refs: whole_kernel(planes, count, *refs), in_specs...  171 us
    unnamed x11, local copies, waits for them, and re-layouts  4.21 us
  transfers between devices with their start and end apart: 2, of which 1 were waited for; matrix products, arithmetic and copies ran while one was open for 0% of the time, Pallas kernels for 0%

profile of v2, /device:TPU:13, one launch (start us, length us, event | category | flops | bytes accessed | tf_op | source)
XLA Modules:
  0.0 189.0 jit_solution(5188556993581537178)
XLA Ops:
  0.6 1.4 copy.21.refs_6_
  2.0 1.4 copy.20.refs_3_
  3.4 171.4 %whole.1 = (f32[1,2,8,128,128]{4,3,2,1,0:T(8,128)}, f32[1,8,128,128]{3,2,1,0:T(8,128)}) custom-call(bf16[1,4,8,128,128]{4,3,2,1,0:T(8,128)(2,1)} %refs_0_.1, f32[1,8,128,128]{3,2,1,0:T(8,128)} %refs_1_.1, bf16[5,128]{1,0:T(8,128)(2,1)} %refs_2_.1, bf16[128,32]{1,0:T(8,128)(2,1)} %copy.20.refs_3_, bf16[2,32,32]{2,1,0:T(8,128)(2,1)} %refs_4_.1, ...), custom_call_target="tpu_custom_call" | custom-call | tf_op jit(solution)/shard_map/whole/pallas_call | solution.py:619
  174.8 0.0 copy-start
  174.8 1.1 convert_bitcast_fusion.4
  175.9 0.0 copy-start.1
  175.9 1.2 fusion.30
  177.2 0.0 copy-start.2
  177.2 1.9 %collective-permute-start = (bf16[1,2,1,128,128]{4,3,2,1,0:T(8,128)(2,1)S(1)}, bf16[1,2,1,128,128]{4,3,2,1,0:T(8,128)(2,1)S(1)}, u32[]{:S(2)}, u32[]{:S(2)}) collective-permute-start(bf16[1,2,1,128,128]{4,3,2,1,0:T(8,128)(2,1)S(1)} %get-tuple-element.16), channel_id=1, source_target_pairs={{0,1},{1,2},{2,3},{3,4},{4,5},{5,6},{6,7},{7,8},{8,9},{9,10},{10,1... | collective-permute-start | bytes 196616 | tf_op jit(solution)/shard_map/ppermute | solution.py:28
  179.1 2.4 %collective-permute-start.1 = (bf16[1,2,1,128,128]{4,3,2,1,0:T(8,128)(2,1)S(1)}, bf16[1,2,1,128,128]{4,3,2,1,0:T(8,128)(2,1)S(1)}, u32[]{:S(2)}, u32[]{:S(2)}) collective-permute-start(bf16[1,2,1,128,128]{4,3,2,1,0:T(8,128)(2,1)S(1)} %get-tuple-element.17), channel_id=1, source_target_pairs={{1,0},{2,1},{3,2},{4,3},{5,4},{6,5},{7,6},{8,7},{9,8},{10,9},{11,1... | collective-permute-start | bytes 196616 | tf_op jit(solution)/shard_map/ppermute | solution.py:31
  181.6 0.0 copy-done
  181.6 0.0 copy-done.1
  181.7 0.0 copy-done.2
  181.7 0.1 fusion.23
  181.8 0.0 copy-start.3
  181.8 0.2 fusion.31
  182.0 0.5 copy-done.3
  182.4 0.1 fusion.22
  182.5 0.1 broadcast_multiply_fusion
  182.6 0.1 maximum_bitcast_fusion
  182.7 0.0 collective-permute-done
  182.7 2.9 %collective-permute-done.1 = bf16[1,2,1,128,128]{4,3,2,1,0:T(8,128)(2,1)S(1)} collective-permute-done((bf16[1,2,1,128,128]{4,3,2,1,0:T(8,128)(2,1)S(1)}, bf16[1,2,1,128,128]{4,3,2,1,0:T(8,128)(2,1)S(1)}, u32[]{:S(2)}, u32[]{:S(2)}) %collective-permute-start.1) | collective-permute-done | bytes 65568 | tf_op jit(solution)/shard_map/ppermute | solution.py:31
  185.7 2.4 %fusion = f32[1,8,128,128]{3,2,1,0:T(8,128)} fusion(f32[1,8,128,128]{3,2,1,0:T(8,128)S(1)} %slice_bitcast_fusion, f32[1,7,128,128]{3,2,1,0:T(8,128)S(1)} %get-tuple-element.21, f32[1,1,128,128]{3,2,1,0:T(8,128)S(1)} %get-tuple-element.10, f32[1,1,128,128]{3,2,1,0:T(8,128)S(1)} %get-tuple-element.11, f32[1,7,128,128]{3,2,1,0:T(8,128)S(1)} %get-tuple-element.22, ...), kind=kOutput, calls=%fused_computation.9 | convolution fusion | flops 55709696 | bytes 3801216 | tf_op jit(solution)/shard_map/bwa,bwz->baz/dot_general | solution.py:133
  188.0 1.0 copy.33
  (5 shorter events, 0.1 us)
Async XLA Ops:
  174.8 6.8 %copy-start = (f32[1,8,128,128]{3,2,1,0:T(8,128)S(1)}, f32[1,8,128,128]{3,2,1,0:T(8,128)}, u32[]{:S(2)}) copy-start(f32[1,8,128,128]{3,2,1,0:T(8,128)} %get-tuple-element.5) | copy-start | bytes 1572868
  175.9 5.7 %copy-start.1 = (f32[1,2,8,128,128]{4,3,2,1,0:T(8,128)S(1)}, f32[1,2,8,128,128]{4,3,2,1,0:T(8,128)}, u32[]{:S(2)}) copy-start(f32[1,2,8,128,128]{4,3,2,1,0:T(8,128)} %get-tuple-element.25) | copy-start | bytes 3145732
  177.2 4.5 %copy-start.2 = (s32[1,32]{1,0:T(1,128)S(1)}, s32[1,32]{1,0:T(1,128)}, u32[]{:S(2)}) copy-start(s32[1,32]{1,0:T(1,128)} %param.18) | copy-start | bytes 388
  177.2 5.5 %collective-permute-start = (bf16[1,2,1,128,128]{4,3,2,1,0:T(8,128)(2,1)S(1)}, bf16[1,2,1,128,128]{4,3,2,1,0:T(8,128)(2,1)S(1)}, u32[]{:S(2)}, u32[]{:S(2)}) collective-permute-start(bf16[1,2,1,128,128]{4,3,2,1,0:T(8,128)(2,1)S(1)} %get-tuple-element.16), channel_id=1, source_target_pairs={{0,1},{1,2},{2,3},{3,4},{4,5},{5,6},{6,7},{7,8},{8,9},{9,10},{10,1... | collective-permute-start | bytes 196616 | tf_op jit(solution)/shard_map/ppermute | solution.py:28
  179.1 6.5 %collective-permute-start.1 = (bf16[1,2,1,128,128]{4,3,2,1,0:T(8,128)(2,1)S(1)}, bf16[1,2,1,128,128]{4,3,2,1,0:T(8,128)(2,1)S(1)}, u32[]{:S(2)}, u32[]{:S(2)}) collective-permute-start(bf16[1,2,1,128,128]{4,3,2,1,0:T(8,128)(2,1)S(1)} %get-tuple-element.17), channel_id=1, source_target_pairs={{1,0},{2,1},{3,2},{4,3},{5,4},{6,5},{7,6},{8,7},{9,8},{10,9},{11,1... | collective-permute-start | bytes 196616 | tf_op jit(solution)/shard_map/ppermute | solution.py:31
  181.8 0.7 copy-start.3
